TPU v7x, 128 devices: a whole 4x4x4 slice. The times are simulated.
128 devices in a mesh: sa: 4 (over x), sb: 2 (over core), sc: 16 (over z, y).
Axes of the slice: x: 4, y: 4, z: 4, core: 2. Of those that a mesh axis runs over, the one named last changes fastest.
Arguments:
- queries: float32 [65536, 2048], P(('sa', 'sb', 'sc')), may hold values from -6 to 6
- key_rows: float32 [65536, 2048], P(('sa', 'sb', 'sc')), may hold values from -6 to 6
- value_rows: float32 [65536, 2048], P(('sa', 'sb', 'sc')), may hold values from -6 to 6
- out_grad: float32 [65536, 2048], P(('sa', 'sb', 'sc')), may hold values from -6 to 6
- prefix_state: float32 [16, 128, 128], replicated, may hold values from -1536 to 1536
- suffix_state: float32 [16, 128, 128], replicated, may hold values from -1536 to 1536
Outputs:
- query_grad: bfloat16 [65536, 2048], P(('sa', 'sb', 'sc'))
- key_grad: bfloat16 [65536, 2048], P(('sa', 'sb', 'sc'))
- value_grad: bfloat16 [65536, 2048], P(('sa', 'sb', 'sc'))
All inputs are finite; a program needn't handle non-finite values.
Results may differ from a plain program's by a relative error of at most 0.0019.
Values sent between devices are 32-bit elements; how exact they have to be, the bound alone decides.
A program may use at most 576 MiB of HBM per device.

v0:
```python
import math
import jax
import jax.numpy as jnp
from jax import lax
from jax.sharding import PartitionSpec as P


def entering(part, axis, combine, identity):
    place = lax.axis_index(axis)
    gathered = jax.tree.map(lambda a: lax.all_gather(a, axis), part)
    state = jax.tree.map(lambda a, e: jnp.zeros_like(a) + jnp.asarray(e, a.dtype), part, identity)

    def one(hop, state):
        return combine(
            state, jax.tree.map(lambda a: lax.dynamic_index_in_dim(a, hop, 0, False), gathered)
        )

    return lax.fori_loop(0, place, one, state)


def add_states(earlier, later):
    return jax.tree.map(lambda left, right: left + right, earlier, later)


def run_chain(local_terms):
    zero_state = jax.tree.map(jnp.zeros_like, local_terms)
    inner_part = entering(local_terms, "sc", add_states, zero_state)
    group_sum = lax.psum((local_terms[0], local_terms[1]), "sc")
    middle_part = entering(group_sum, "sb", add_states, zero_state)
    block_sum = lax.psum((group_sum[0], group_sum[1]), "sb")
    outer_part = entering(block_sum, "sa", add_states, zero_state)
    return add_states(add_states(outer_part, middle_part), inner_part)


def shards(queries, key_rows, value_rows, out_grad, prefix_state, suffix_state):
    row_count = queries.shape[0]
    head_count = prefix_state.shape[0]
    head_size = prefix_state.shape[1]
    device_count = lax.axis_size("sa") * lax.axis_size("sb") * lax.axis_size("sc")
    factor = 1.0 / math.sqrt(head_size * row_count * device_count)
    highest = lax.Precision.HIGHEST
    shaped = (row_count, head_count, head_size)
    query_t = queries.reshape(shaped)
    key_t = key_rows.reshape(shaped)
    value_t = value_rows.reshape(shaped)
    grad_t = out_grad.reshape(shaped)
    kv_local = jnp.einsum("thd,the->hde", key_t, value_t, precision=highest)
    grad_local = jnp.einsum("the,thd->hed", grad_t, query_t, precision=highest)
    prior_kv, prior_grad = run_chain((kv_local, grad_local))
    total_grad = lax.psum(grad_local, ("sa", "sb", "sc"))
    state_before = prefix_state + prior_kv
    state_after = suffix_state + (total_grad - prior_grad - grad_local)
    lower = (
        lax.broadcasted_iota(jnp.int32, (row_count, row_count), 0)
        >= lax.broadcasted_iota(jnp.int32, (row_count, row_count), 1)
    ).astype(jnp.float32)
    grad_scores = jnp.einsum("the,she->hts", grad_t, value_t, precision=highest) * lower
    attn_scores = jnp.einsum("thd,shd->hts", query_t, key_t, precision=highest) * lower
    query_grad = factor * (
        jnp.einsum("the,hde->thd", grad_t, state_before, precision=highest)
        + jnp.einsum("hts,shd->thd", grad_scores, key_t, precision=highest)
    )
    key_grad = factor * (
        jnp.einsum("she,hed->shd", value_t, state_after, precision=highest)
        + jnp.einsum("hts,thd->shd", grad_scores, query_t, precision=highest)
    )
    value_grad = factor * (
        jnp.einsum("shd,hed->she", key_t, state_after, precision=highest)
        + jnp.einsum("hts,the->she", attn_scores, grad_t, precision=highest)
    )
    flat = (row_count, head_count * head_size)
    return (
        query_grad.astype(jnp.bfloat16).reshape(flat),
        key_grad.astype(jnp.bfloat16).reshape(flat),
        value_grad.astype(jnp.bfloat16).reshape(flat),
    )


def solution(mesh):
    return jax.shard_map(
        shards,
        mesh=mesh,
        in_specs=(
            P(("sa", "sb", "sc"), None),
            P(("sa", "sb", "sc"), None),
            P(("sa", "sb", "sc"), None),
            P(("sa", "sb", "sc"), None),
            P(),
            P(),
        ),
        out_specs=(
            P(("sa", "sb", "sc"), None),
            P(("sa", "sb", "sc"), None),
            P(("sa", "sb", "sc"), None),
        ),
        check_vma=False,
    )
```

profile of v0, /device:TPU:1, one launch (start us, length us, event | category | flops | bytes accessed | tf_op | source)
XLA Modules:
  0.0 613.8 jit_solution(8954921210702635121)
XLA Ops:
  8.0 0.0 all-gather.19.cloned.1.call-start
  8.0 11.2 %fusion.21 = f32[16,128,128]{2,1,0:T(8,128)} fusion(f32[512,2048]{1,0:T(8,128)} %param.14, f32[512,2048]{1,0:T(8,128)} %param.13), kind=kOutput, calls=%fused_computation.27 | convolution fusion | flops 1610612736 | bytes 9437184 | tf_op jit(solution)/shard_map/thd,the->hde/dot_general | solution.py:47
  19.2 5.1 copy.46
  24.3 5.7 copy.27
  30.1 9.2 %fusion.16 = f32[16,128,128]{2,1,0:T(8,128)} fusion(f32[512,16,128]{0,2,1:T(8,128)} %copy.27, f32[512,2048]{1,0:T(8,128)} %param.12), kind=kOutput, calls=%fused_computation.22 | convolution fusion | flops 1610612736 | bytes 9437184 | tf_op jit(solution)/shard_map/the,thd->hed/dot_general | solution.py:48
  39.3 94.8 %all-gather.19.cloned.1.call-done = f32[256,128,128]{2,1,0:T(8,128)} async-done(((f32[16,128,128]{2,1,0:T(8,128)}), f32[256,128,128]{2,1,0:T(8,128)}) %all-gather.19.cloned.1.call-update) | async-done | bytes 16777232 | tf_op jit(solution)/shard_map/all_gather | solution.py:10
  134.0 0.7 all-reduce.8.cloned.1.call-update
  134.8 0.0 all-gather.15.cloned.1.call-start
  134.8 93.1 %all-reduce.8.cloned.1.call-done = (f32[16,128,128]{2,1,0:T(8,128)}, f32[16,128,128]{2,1,0:T(8,128)}) async-done(((f32[16,128,128]{2,1,0:T(8,128)}, f32[16,128,128]{2,1,0:T(8,128)}), (f32[16,128,128]{2,1,0:T(8,128)}, f32[16,128,128]{2,1,0:T(8,128)})) %all-reduce.8.cloned.1.call-update) | async-done | bytes 2097168 | tf_op jit(solution)/shard_map/psum | solution.py:28
  228.0 0.0 all-gather.17.cloned.1.call-start
  228.0 0.5 all-gather.17.cloned.1.call-update
  228.5 15.4 %all-gather.15.cloned.1.call-done = f32[32,128,128]{2,1,0:T(8,128)} async-done(((f32[16,128,128]{2,1,0:T(8,128)}), f32[32,128,128]{2,1,0:T(8,128)}) %all-gather.15.cloned.1.call-update) | async-done | bytes 2097168 | tf_op jit(solution)/shard_map/all_gather | solution.py:10
  243.9 16.3 %all-gather.17.cloned.1.call-done = f32[32,128,128]{2,1,0:T(8,128)} async-done(((f32[16,128,128]{2,1,0:T(8,128)}), f32[32,128,128]{2,1,0:T(8,128)}) %all-gather.17.cloned.1.call-update) | async-done | bytes 2097168 | tf_op jit(solution)/shard_map/all_gather | solution.py:10
  260.2 0.6 all-reduce.10.cloned.1.call-update
  260.8 0.0 all-gather.21.cloned.1.call-start
  260.8 0.5 all-gather.21.cloned.1.call-update
  261.4 30.2 %all-reduce.10.cloned.1.call-done = (f32[1,16,128,128]{3,2,1,0:T(8,128)}, f32[1,16,128,128]{3,2,1,0:T(8,128)}) async-done(((f32[1,16,128,128]{3,2,1,0:T(8,128)}, f32[1,16,128,128]{3,2,1,0:T(8,128)}), (f32[1,16,128,128]{3,2,1,0:T(8,128)}, f32[1,16,128,128]{3,2,1,0:T(8,128)})) %all-reduce.10.cloned.1.call-update) | async-done | bytes 2097168 | tf_op jit(solution)/shard_map/psum | solution.py:30
  291.6 0.0 all-gather.13.cloned.1.call-start
  291.6 0.7 all-gather.13.cloned.1.call-update
  292.3 0.0 all-reduce.6.cloned.1.call-start
  292.4 0.5 all-reduce.6.cloned.1.call-update
  292.9 0.1 fusion.55
  293.1 19.5 %fusion.14 = f32[16,512,512]{2,1,0:T(8,128)} fusion(f32[512,2048]{1,0:T(8,128)} %param.12, f32[512,2048]{1,0:T(8,128)} %param.13), kind=kOutput, calls=%fused_computation.20 | convolution fusion | flops 6442450944 | bytes 25165824 | tf_op jit(solution)/shard_map/thd,shd->hts/dot_general | solution.py:58
  312.6 14.5 %fusion.11 = f32[16,512,512]{2,1,0:T(8,128)S(1)} fusion(f32[512,2048]{1,0:T(8,128)S(1)} %copy-done.4, f32[512,2048]{1,0:T(8,128)S(1)} %copy-done.5), kind=kOutput, calls=%fused_computation.17 | convolution fusion | flops 6442450944 | bytes 25165824 | tf_op jit(solution)/shard_map/the,she->hts/dot_general | solution.py:57
  327.1 14.5 %fusion.2 = f32[16,512,128]{1,2,0:T(8,128)} fusion(f32[16,512,512]{2,1,0:T(8,128)S(1)} %fusion.11, f32[512,512]{1,0:T(8,128)S(1)} %fusion.55, f32[512,2048]{1,0:T(8,128)} %param.12), kind=kOutput, calls=%fused_computation.8 | convolution fusion | flops 6446645248 | bytes 26214400 | tf_op jit(solution)/shard_map/hts,thd->shd/dot_general | solution.py:65
  341.6 21.3 %fusion.4 = f32[16,512,128]{1,2,0:T(8,128)} fusion(f32[16,512,512]{2,1,0:T(8,128)S(1)} %fusion.11, f32[512,512]{1,0:T(8,128)S(1)} %fusion.55, f32[512,2048]{1,0:T(8,128)} %param.13), kind=kOutput, calls=%fused_computation.10 | convolution fusion | flops 6446645248 | bytes 26214400 | tf_op jit(solution)/shard_map/hts,shd->thd/dot_general | solution.py:61
  362.9 44.5 %all-gather.21.cloned.1.call-done = f32[256,128,128]{2,1,0:T(8,128)} async-done(((f32[16,128,128]{2,1,0:T(8,128)}), f32[256,128,128]{2,1,0:T(8,128)}) %all-gather.21.cloned.1.call-update) | async-done | bytes 16777232 | tf_op jit(solution)/shard_map/all_gather | solution.py:10
  407.4 0.1 broadcast.6.clone
  407.5 0.1 broadcast.6.clone.1
  407.6 1.0 copy-done.1
  408.6 0.1 broadcast.6.clone.4
  408.7 0.1 broadcast.6.clone.5
  408.8 2.1 while.37
  408.8 2.1 bitcast_add_fusion.13
  410.9 45.8 %all-gather.11.cloned.1.call-done = f32[4,16,128,128]{3,2,1,0:T(8,128)} async-done(((f32[1,16,128,128]{3,2,1,0:T(8,128)}), f32[4,16,128,128]{3,2,1,0:T(8,128)}) %all-gather.11.cloned.1.call-update) | async-done | bytes 4194320 | tf_op jit(solution)/shard_map/all_gather | solution.py:10
  456.7 50.5 %all-gather.13.cloned.1.call-done = f32[4,16,128,128]{3,2,1,0:T(8,128)} async-done(((f32[1,16,128,128]{3,2,1,0:T(8,128)}), f32[4,16,128,128]{3,2,1,0:T(8,128)}) %all-gather.13.cloned.1.call-update) | async-done | bytes 4194320 | tf_op jit(solution)/shard_map/all_gather | solution.py:10
  507.2 0.1 broadcast.6.clone.2
  507.3 1.1 broadcast.6.clone.3
  508.4 44.6 %all-reduce.6.cloned.1.call-done = f32[16,128,128]{2,1,0:T(8,128)} async-done(((f32[16,128,128]{2,1,0:T(8,128)}), f32[16,128,128]{2,1,0:T(8,128)}) %all-reduce.6.cloned.1.call-update) | async-done | bytes 1048592 | tf_op jit(solution)/shard_map/psum | solution.py:50
  552.9 3.5 subtract_add_fusion
  556.4 1.0 copy-done.8
  557.5 3.8 fusion.23
  561.3 14.6 %fusion.29 = bf16[512,16,128]{0,2,1:T(8,128)(2,1)} fusion(f32[16,128,512]{2,1,0:T(8,128)S(1)} %fusion.23, f32[512,16,128]{0,2,1:T(8,128)S(1)} %copy-done.3, f32[16,512,512]{2,1,0:T(8,128)} %fusion.14, f32[512,512]{1,0:T(8,128)S(1)} %copy-done.7), kind=kOutput, calls=%fused_computation.36 | convolution fusion | flops 6449790976 | bytes 28311552 | tf_op jit(solution)/shard_map/hts,the->she/dot_general | solution.py:69
  575.9 3.9 copy.40
  579.8 9.2 %fusion.31 = bf16[512,16,128]{0,2,1:T(8,128)(2,1)} fusion(f32[16,512,128]{1,2,0:T(8,128)} %fusion.2, f32[16,128,128]{2,1,0:T(8,128)} %copy-done.8, f32[512,2048]{1,0:T(8,128)} %param.14), kind=kOutput, calls=%fused_computation.39 | convolution fusion | flops 1613758464 | bytes 11534336 | tf_op jit(solution)/shard_map/she,hed->shd/dot_general | solution.py:64
  589.0 4.1 copy.39
  593.1 9.2 %fusion.33 = bf16[512,16,128]{0,2,1:T(8,128)(2,1)} fusion(f32[16,512,128]{1,2,0:T(8,128)} %fusion.4, f32[16,128,128]{2,1,0:T(8,128)} %param.16, f32[16,128,128]{2,1,0:T(8,128)S(1)} %get-tuple-element.107, f32[16,128,128]{2,1,0:T(8,128)S(1)} %get-tuple-element.105, f32[16,128,128]{2,1,0:T(8,128)S(1)} %get-tuple-element.106, f32[512,2048]{1,0:T(8,128)} %param.15), kind=kOutput, calls=%fused_computation.42 | convolution fusion | flops 1614544896 | bytes 14680064 | tf_op jit(solution)/shard_map/the,hde->thd/dot_general | solution.py:60
  602.3 3.9 copy.38
  (24 shorter events, 0.1 us)
Async XLA Ops:
  8.0 126.0 %all-gather.19.cloned.1.call-start = ((), (), s32[]{:S(2)}) async-start(), calls=%async_computation.5 | async-start | bytes 17825792 | tf_op jit(solution)/shard_map/all_gather | solution.py:10
  134.0 93.9 %all-reduce.8.cloned.1.call-start = ((), (), s32[]{:S(2)}) async-start(), calls=%async_computation.7 | async-start | bytes 4194304 | tf_op jit(solution)/shard_map/psum | solution.py:28
  134.8 109.2 %all-gather.15.cloned.1.call-start = ((), (), s32[]{:S(2)}) async-start(), calls=%async_computation.3 | async-start | bytes 3145728 | tf_op jit(solution)/shard_map/all_gather | solution.py:10
  228.0 32.2 %all-gather.17.cloned.1.call-start = ((), (), s32[]{:S(2)}) async-start(), calls=%async_computation.4 | async-start | bytes 3145728 | tf_op jit(solution)/shard_map/all_gather | solution.py:10
  260.2 31.4 %all-reduce.10.cloned.1.call-start = ((), (), s32[]{:S(2)}) async-start(), calls=%async_computation.8 | async-start | bytes 4194304 | tf_op jit(solution)/shard_map/psum | solution.py:30
  260.8 146.6 %all-gather.21.cloned.1.call-start = ((), (), s32[]{:S(2)}) async-start(), calls=%async_computation.6 | async-start | bytes 17825792 | tf_op jit(solution)/shard_map/all_gather | solution.py:10
  261.4 195.3 %all-gather.11.cloned.1.call-start = ((), (), s32[]{:S(2)}) async-start(), calls=%async_computation | async-start | bytes 5242880 | tf_op jit(solution)/shard_map/all_gather | solution.py:10
  291.6 215.6 %all-gather.13.cloned.1.call-start = ((), (), s32[]{:S(2)}) async-start(), calls=%async_computation.1 | async-start | bytes 5242880 | tf_op jit(solution)/shard_map/all_gather | solution.py:10
  292.3 260.6 %all-reduce.6.cloned.1.call-start = ((), (), s32[]{:S(2)}) async-start(), calls=%async_computation.2 | async-start | bytes 2097152 | tf_op jit(solution)/shard_map/psum | solution.py:50
  293.0 48.6 %copy-start.6 = (f32[512,512]{1,0:T(8,128)}, f32[512,512]{1,0:T(8,128)S(1)}, u32[]{:S(2)}) copy-start(f32[512,512]{1,0:T(8,128)S(1)} %fusion.55) | copy-start | bytes 3145732
  293.1 19.6 %copy-start.4 = (f32[512,2048]{1,0:T(8,128)S(1)}, f32[512,2048]{1,0:T(8,128)}, u32[]{:S(2)}) copy-start(f32[512,2048]{1,0:T(8,128)} %param.15) | copy-start | bytes 12582916
  293.1 19.6 %copy-start.5 = (f32[512,2048]{1,0:T(8,128)S(1)}, f32[512,2048]{1,0:T(8,128)}, u32[]{:S(2)}) copy-start(f32[512,2048]{1,0:T(8,128)} %param.14) | copy-start | bytes 12582916
  407.6 1.0 copy-start.1
  410.9 45.8 %copy-start.2 = (f32[16,128,128]{2,1,0:T(8,128)}, f32[16,128,128]{2,1,0:T(8,128)S(1)}, u32[]{:S(2)}) copy-start(f32[16,128,128]{2,1,0:T(8,128)S(1)} %get-tuple-element.109) | copy-start | bytes 3145732
  552.9 4.5 copy-start
  556.4 1.0 copy-start.8
  557.5 3.8 copy-start.3
  557.5 3.8 copy-start.7
Sparse Core Ops, SparseCore 0:
  19.4 114.6 all-gather.18
  138.8 89.0 all-reduce.7
  229.7 14.2 all-gather.14
  245.5 14.6 all-gather.16
  263.4 28.1 all-reduce.9
  294.1 113.1 all-gather.20
  409.0 47.6 all-gather.10
  458.3 48.7 all-gather.12
Sparse Core Ops, SparseCore 1:
  298.2 254.7 all-reduce.5
where the time goes:
time: 621 us; the launch traced here: 614 us
  waiting for transfers between devices  439 us (71%)
  matrix products  127 us (20%)
  local copies, waits for them, and re-layouts  26.3 us (4%)
  between operations  16 us (3%)
    all_gather x6, waiting for transfers between devices, entering(): gathered = jax.tree.map(lambda a: lax.all_gather(a, axis), part)  267 us
    psum x1, waiting for transfers between devices, run_chain(): group_sum = lax.psum((local_terms[0], local_terms[1]), 'sc')  93.1 us
    psum x1, waiting for transfers between devices, shards(): total_grad = lax.psum(grad_local, ('sa', 'sb', 'sc'))  44.6 us
    psum x1, waiting for transfers between devices, run_chain(): block_sum = lax.psum((group_sum[0], group_sum[1]), 'sb')  30.2 us
    dot_general x1, matrix products, shards(): jnp.einsum('hts,shd->thd', grad_scores, key_t, precision=highest)  21.3 us
    dot_general x1, matrix products, shards(): jnp.einsum('thd,shd->hts', query_t, key_t, precision=highest) * lower  19.5 us
    unnamed x22, local copies, waits for them, and re-layouts  19 us
    dot_general x1, matrix products, shards(): jnp.einsum('hts,the->she', attn_scores, grad_t, precision=highest)  14.6 us
  transfers between devices with their start and end apart: 9, of which 9 were waited for; matrix products, arithmetic and copies ran while one was open for 15% of the time, Pallas kernels for 0%

commit v1 on v0

--- a/solution.py
+++ b/solution.py
@@ -47,7 +47,7 @@
     kv_local = jnp.einsum("thd,the->hde", key_t, value_t, precision=highest)
     grad_local = jnp.einsum("the,thd->hed", grad_t, query_t, precision=highest)
     prior_kv, prior_grad = run_chain((kv_local, grad_local))
-    total_grad = lax.psum(grad_local, ("sa", "sb", "sc"))
+    total_grad = lax.psum(lax.psum(grad_local, "sa"), ("sb", "sc"))
     state_before = prefix_state + prior_kv
     state_after = suffix_state + (total_grad - prior_grad - grad_local)
     lower = (

time: 621 us -> 732 us (1.18)
  waiting for transfers between devices: 439 us -> 551 us
    psum x1 -> x2, waiting for transfers between devices: 44.6 us -> 108 us  [shards(): total_grad = lax.psum(lax.psum(grad_local, 'sa'), ('sb', 'sc'))]
    all_gather x6, waiting for transfers between devices: 267 us -> 317 us  [entering(): gathered = jax.tree.map(lambda a: lax.all_gather(a, axis), part)]
  transfers between devices with their start and end apart: 9 -> 10, of which waited for: 9 -> 9; matrix products, arithmetic and copies ran while one was open for 15% -> 13% of each run, Pallas kernels for 0% -> 0%
where the time goes in v1:
time: 732 us; the launch traced here: 725 us
  waiting for transfers between devices  551 us (75%)
  matrix products  127 us (17%)
  local copies, waits for them, and re-layouts  26.3 us (4%)
  between operations  14.6 us (2%)
    all_gather x6, waiting for transfers between devices, entering(): gathered = jax.tree.map(lambda a: lax.all_gather(a, axis), part)  317 us
    psum x2, waiting for transfers between devices, shards(): total_grad = lax.psum(lax.psum(grad_local, 'sa'), ('sb', 'sc'))  108 us
    psum x1, waiting for transfers between devices, run_chain(): group_sum = lax.psum((local_terms[0], local_terms[1]), 'sc')  93.1 us
    psum x1, waiting for transfers between devices, run_chain(): block_sum = lax.psum((group_sum[0], group_sum[1]), 'sb')  29.4 us
    dot_general x1, matrix products, shards(): jnp.einsum('hts,shd->thd', grad_scores, key_t, precision=highest)  21 us
    dot_general x1, matrix products, shards(): jnp.einsum('thd,shd->hts', query_t, key_t, precision=highest) * lower  19.5 us
    unnamed x22, local copies, waits for them, and re-layouts  19 us
    dot_general x1, matrix products, shards(): jnp.einsum('hts,thd->shd', grad_scores, query_t, precision=highest)  14.8 us
  transfers between devices with their start and end apart: 10, of which 9 were waited for; matrix products, arithmetic and copies ran while one was open for 13% of the time, Pallas kernels for 0%

profile of v1, /device:TPU:1, one launch (start us, length us, event | category | flops | bytes accessed | tf_op | source)
XLA Modules:
  0.0 724.6 jit_solution(9599324191952776128)
XLA Ops:
  7.2 0.0 all-gather.19.cloned.1.call-start
  7.2 11.2 %fusion.21 = f32[16,128,128]{2,1,0:T(8,128)} fusion(f32[512,2048]{1,0:T(8,128)} %param.14, f32[512,2048]{1,0:T(8,128)} %param.13), kind=kOutput, calls=%fused_computation.27 | convolution fusion | flops 1610612736 | bytes 9437184 | tf_op jit(solution)/shard_map/thd,the->hde/dot_general | solution.py:47
  18.4 5.1 copy.46
  23.5 5.7 copy.27
  29.2 9.2 %fusion.16 = f32[16,128,128]{2,1,0:T(8,128)} fusion(f32[512,16,128]{0,2,1:T(8,128)} %copy.27, f32[512,2048]{1,0:T(8,128)} %param.12), kind=kOutput, calls=%fused_computation.22 | convolution fusion | flops 1610612736 | bytes 9437184 | tf_op jit(solution)/shard_map/the,thd->hed/dot_general | solution.py:48
  38.4 94.8 %all-gather.19.cloned.1.call-done = f32[256,128,128]{2,1,0:T(8,128)} async-done(((f32[16,128,128]{2,1,0:T(8,128)}), f32[256,128,128]{2,1,0:T(8,128)}) %all-gather.19.cloned.1.call-update) | async-done | bytes 16777232 | tf_op jit(solution)/shard_map/all_gather | solution.py:10
  133.2 0.7 all-reduce.11.cloned.1.call-update
  133.9 0.0 all-gather.15.cloned.1.call-start
  134.0 93.1 %all-reduce.11.cloned.1.call-done = (f32[16,128,128]{2,1,0:T(8,128)}, f32[16,128,128]{2,1,0:T(8,128)}) async-done(((f32[16,128,128]{2,1,0:T(8,128)}, f32[16,128,128]{2,1,0:T(8,128)}), (f32[16,128,128]{2,1,0:T(8,128)}, f32[16,128,128]{2,1,0:T(8,128)})) %all-reduce.11.cloned.1.call-update) | async-done | bytes 2097168 | tf_op jit(solution)/shard_map/psum | solution.py:28
  227.1 0.0 all-gather.17.cloned.1.call-start
  227.2 0.5 all-gather.17.cloned.1.call-update
  227.7 15.4 %all-gather.15.cloned.1.call-done = f32[32,128,128]{2,1,0:T(8,128)} async-done(((f32[16,128,128]{2,1,0:T(8,128)}), f32[32,128,128]{2,1,0:T(8,128)}) %all-gather.15.cloned.1.call-update) | async-done | bytes 2097168 | tf_op jit(solution)/shard_map/all_gather | solution.py:10
  243.1 16.3 %all-gather.17.cloned.1.call-done = f32[32,128,128]{2,1,0:T(8,128)} async-done(((f32[16,128,128]{2,1,0:T(8,128)}), f32[32,128,128]{2,1,0:T(8,128)}) %all-gather.17.cloned.1.call-update) | async-done | bytes 2097168 | tf_op jit(solution)/shard_map/all_gather | solution.py:10
  259.4 0.6 all-reduce.13.cloned.1.call-update
  259.9 0.0 all-reduce.7.cloned.1.call-start
  260.0 0.5 all-reduce.7.cloned.1.call-update
  260.5 0.0 all-gather.21.cloned.1.call-start
  260.6 0.7 all-gather.21.cloned.1.call-update
  261.3 29.4 %all-reduce.13.cloned.1.call-done = (f32[1,16,128,128]{3,2,1,0:T(8,128)}, f32[1,16,128,128]{3,2,1,0:T(8,128)}) async-done(((f32[1,16,128,128]{3,2,1,0:T(8,128)}, f32[1,16,128,128]{3,2,1,0:T(8,128)}), (f32[1,16,128,128]{3,2,1,0:T(8,128)}, f32[1,16,128,128]{3,2,1,0:T(8,128)})) %all-reduce.13.cloned.1.call-update) | async-done | bytes 2097168 | tf_op jit(solution)/shard_map/psum | solution.py:30
  290.8 0.7 all-gather.13.cloned.1.call-update
  291.5 0.0 all-reduce.9.cloned.1.call-start
  291.6 0.1 fusion.55
  291.7 19.5 %fusion.14 = f32[16,512,512]{2,1,0:T(8,128)} fusion(f32[512,2048]{1,0:T(8,128)} %param.12, f32[512,2048]{1,0:T(8,128)} %param.13), kind=kOutput, calls=%fused_computation.20 | convolution fusion | flops 6442450944 | bytes 25165824 | tf_op jit(solution)/shard_map/thd,shd->hts/dot_general | solution.py:58
  311.3 14.5 %fusion.11 = f32[16,512,512]{2,1,0:T(8,128)S(1)} fusion(f32[512,2048]{1,0:T(8,128)S(1)} %copy-done.4, f32[512,2048]{1,0:T(8,128)S(1)} %copy-done.5), kind=kOutput, calls=%fused_computation.17 | convolution fusion | flops 6442450944 | bytes 25165824 | tf_op jit(solution)/shard_map/the,she->hts/dot_general | solution.py:57
  325.7 21.0 %fusion.4 = f32[16,512,128]{1,2,0:T(8,128)} fusion(f32[16,512,512]{2,1,0:T(8,128)S(1)} %fusion.11, f32[512,512]{1,0:T(8,128)S(1)} %fusion.55, f32[512,2048]{1,0:T(8,128)} %param.13), kind=kOutput, calls=%fused_computation.10 | convolution fusion | flops 6446645248 | bytes 26214400 | tf_op jit(solution)/shard_map/hts,shd->thd/dot_general | solution.py:61
  346.7 14.8 %fusion.2 = f32[16,512,128]{1,2,0:T(8,128)} fusion(f32[16,512,512]{2,1,0:T(8,128)S(1)} %fusion.11, f32[512,512]{1,0:T(8,128)S(1)} %fusion.55, f32[512,2048]{1,0:T(8,128)} %param.12), kind=kOutput, calls=%fused_computation.8 | convolution fusion | flops 6446645248 | bytes 26214400 | tf_op jit(solution)/shard_map/hts,thd->shd/dot_general | solution.py:65
  361.6 93.9 %all-gather.21.cloned.1.call-done = f32[256,128,128]{2,1,0:T(8,128)} async-done(((f32[16,128,128]{2,1,0:T(8,128)}), f32[256,128,128]{2,1,0:T(8,128)}) %all-gather.21.cloned.1.call-update) | async-done | bytes 16777232 | tf_op jit(solution)/shard_map/all_gather | solution.py:10
  455.5 0.1 broadcast.6.clone
  455.6 0.1 broadcast.6.clone.1
  455.7 1.0 copy-done.1
  456.7 0.1 broadcast.6.clone.4
  456.8 0.1 broadcast.6.clone.5
  456.9 2.1 while.37
  456.9 2.1 bitcast_add_fusion.13
  459.0 46.1 %all-gather.11.cloned.1.call-done = f32[4,16,128,128]{3,2,1,0:T(8,128)} async-done(((f32[1,16,128,128]{3,2,1,0:T(8,128)}), f32[4,16,128,128]{3,2,1,0:T(8,128)}) %all-gather.11.cloned.1.call-update) | async-done | bytes 4194320 | tf_op jit(solution)/shard_map/all_gather | solution.py:10
  505.1 50.4 %all-gather.13.cloned.1.call-done = f32[4,16,128,128]{3,2,1,0:T(8,128)} async-done(((f32[1,16,128,128]{3,2,1,0:T(8,128)}), f32[4,16,128,128]{3,2,1,0:T(8,128)}) %all-gather.13.cloned.1.call-update) | async-done | bytes 4194320 | tf_op jit(solution)/shard_map/all_gather | solution.py:10
  555.5 0.1 broadcast.6.clone.2
  555.6 1.1 broadcast.6.clone.3
  556.7 107.6 %all-reduce.9.cloned.1.call-done = f32[16,128,128]{2,1,0:T(8,128)} async-done(((f32[16,128,128]{2,1,0:T(8,128)}), f32[16,128,128]{2,1,0:T(8,128)}) %all-reduce.9.cloned.1.call-update) | async-done | bytes 1048592 | tf_op jit(solution)/shard_map/psum | solution.py:50
  664.3 3.5 subtract_add_fusion
  667.8 1.0 copy-done.8
  668.8 3.8 fusion.23
  672.6 14.6 %fusion.29 = bf16[512,16,128]{0,2,1:T(8,128)(2,1)} fusion(f32[16,128,512]{2,1,0:T(8,128)S(1)} %fusion.23, f32[512,16,128]{0,2,1:T(8,128)S(1)} %copy-done.3, f32[16,512,512]{2,1,0:T(8,128)} %fusion.14, f32[512,512]{1,0:T(8,128)S(1)} %copy-done.7), kind=kOutput, calls=%fused_computation.36 | convolution fusion | flops 6449790976 | bytes 28311552 | tf_op jit(solution)/shard_map/hts,the->she/dot_general | solution.py:69
  687.2 3.9 copy.40
  691.2 9.2 %fusion.31 = bf16[512,16,128]{0,2,1:T(8,128)(2,1)} fusion(f32[16,512,128]{1,2,0:T(8,128)} %fusion.2, f32[16,128,128]{2,1,0:T(8,128)} %copy-done.8, f32[512,2048]{1,0:T(8,128)} %param.14), kind=kOutput, calls=%fused_computation.39 | convolution fusion | flops 1613758464 | bytes 11534336 | tf_op jit(solution)/shard_map/she,hed->shd/dot_general | solution.py:64
  700.3 4.1 copy.39
  704.4 9.2 %fusion.33 = bf16[512,16,128]{0,2,1:T(8,128)(2,1)} fusion(f32[16,512,128]{1,2,0:T(8,128)} %fusion.4, f32[16,128,128]{2,1,0:T(8,128)} %param.16, f32[16,128,128]{2,1,0:T(8,128)S(1)} %get-tuple-element.107, f32[16,128,128]{2,1,0:T(8,128)S(1)} %get-tuple-element.105, f32[16,128,128]{2,1,0:T(8,128)S(1)} %get-tuple-element.106, f32[512,2048]{1,0:T(8,128)} %param.15), kind=kOutput, calls=%fused_computation.42 | convolution fusion | flops 1614544896 | bytes 14680064 | tf_op jit(solution)/shard_map/the,hde->thd/dot_general | solution.py:60
  713.6 3.9 copy.38
  (27 shorter events, 0.2 us)
Async XLA Ops:
  7.2 126.0 %all-gather.19.cloned.1.call-start = ((), (), s32[]{:S(2)}) async-start(), calls=%async_computation.6 | async-start | bytes 17825792 | tf_op jit(solution)/shard_map/all_gather | solution.py:10
  133.2 93.9 %all-reduce.11.cloned.1.call-start = ((), (), s32[]{:S(2)}) async-start(), calls=%async_computation.8 | async-start | bytes 4194304 | tf_op jit(solution)/shard_map/psum | solution.py:28
  133.9 109.2 %all-gather.15.cloned.1.call-start = ((), (), s32[]{:S(2)}) async-start(), calls=%async_computation.4 | async-start | bytes 3145728 | tf_op jit(solution)/shard_map/all_gather | solution.py:10
  227.1 32.2 %all-gather.17.cloned.1.call-start = ((), (), s32[]{:S(2)}) async-start(), calls=%async_computation.5 | async-start | bytes 3145728 | tf_op jit(solution)/shard_map/all_gather | solution.py:10
  259.4 31.4 %all-reduce.13.cloned.1.call-start = ((), (), s32[]{:S(2)}) async-start(), calls=%async_computation.9 | async-start | bytes 4194304 | tf_op jit(solution)/shard_map/psum | solution.py:30
  259.9 101.6 %all-reduce.7.cloned.1.call-start = ((), (), s32[]{:S(2)}) async-start(), calls=%async_computation.2 | async-start | bytes 2097152 | tf_op jit(solution)/shard_map/psum | solution.py:50
  260.5 195.0 %all-gather.21.cloned.1.call-start = ((), (), s32[]{:S(2)}) async-start(), calls=%async_computation.7 | async-start | bytes 17825792 | tf_op jit(solution)/shard_map/all_gather | solution.py:10
  261.3 243.9 %all-gather.11.cloned.1.call-start = ((), (), s32[]{:S(2)}) async-start(), calls=%async_computation | async-start | bytes 5242880 | tf_op jit(solution)/shard_map/all_gather | solution.py:10
  290.8 264.8 %all-gather.13.cloned.1.call-start = ((), (), s32[]{:S(2)}) async-start(), calls=%async_computation.1 | async-start | bytes 5242880 | tf_op jit(solution)/shard_map/all_gather | solution.py:10
  291.5 372.8 %all-reduce.9.cloned.1.call-start = ((), (), s32[]{:S(2)}) async-start(), calls=%async_computation.3 | async-start | bytes 2097152 | tf_op jit(solution)/shard_map/psum | solution.py:50
  291.7 55.0 %copy-start.6 = (f32[512,512]{1,0:T(8,128)}, f32[512,512]{1,0:T(8,128)S(1)}, u32[]{:S(2)}) copy-start(f32[512,512]{1,0:T(8,128)S(1)} %fusion.55) | copy-start | bytes 3145732
  291.7 19.6 %copy-start.4 = (f32[512,2048]{1,0:T(8,128)S(1)}, f32[512,2048]{1,0:T(8,128)}, u32[]{:S(2)}) copy-start(f32[512,2048]{1,0:T(8,128)} %param.15) | copy-start | bytes 12582916
  291.7 19.6 %copy-start.5 = (f32[512,2048]{1,0:T(8,128)S(1)}, f32[512,2048]{1,0:T(8,128)}, u32[]{:S(2)}) copy-start(f32[512,2048]{1,0:T(8,128)} %param.14) | copy-start | bytes 12582916
  455.7 1.0 copy-start.1
  459.0 46.1 %copy-start.2 = (f32[16,128,128]{2,1,0:T(8,128)}, f32[16,128,128]{2,1,0:T(8,128)S(1)}, u32[]{:S(2)}) copy-start(f32[16,128,128]{2,1,0:T(8,128)S(1)} %get-tuple-element.109) | copy-start | bytes 3145732
  664.3 4.5 copy-start
  667.8 1.0 copy-start.8
  668.8 3.8 copy-start.3
  668.8 3.8 copy-start.7
Sparse Core Ops, SparseCore 0:
  18.5 114.6 all-gather.18
  138.0 89.0 all-reduce.10
  228.9 14.2 all-gather.14
  244.7 14.6 all-gather.16
  262.5 28.1 all-reduce.12
  293.5 45.2 all-reduce.6
  341.8 113.6 all-gather.20
  457.3 47.8 all-gather.10
  506.9 48.5 all-gather.12
  559.0 105.2 all-reduce.8
